TPU v7x, 256 devices: a whole 4x4x8 slice. The times are simulated.
256 devices in a mesh: sec: 4 (over x), tile: 64 (over y, z, core).
Axes of the slice: x: 4, y: 4, z: 8, core: 2. Of those that a mesh axis runs over, the one named last changes fastest.
Arguments:
- patches: bfloat16 [4, 256, 512, 512], P('sec', 'tile'), may hold values from -6 to 6
- zoom: float32 [4, 2, 256], P('sec'), may hold values from 0.75 to 0.9
- frac: float32 [4, 2, 256], P('sec'), may hold values from 0 to 1
- offset: int32 [4, 2, 256], P('sec'), may hold values from 0 to 15
- owner: int32 [4, 256, 16, 1], P('sec'), may hold values from 0 to 63; in each aligned block of 64 rows (0 to 63, 64 to 127, ..., all dimensions but the last counted through in order) at most 2 rows name the same one
- top_grid: bfloat16 [64, 256, 256], P('tile'), may hold values from -3 to 3
Outputs:
- grid_image: bfloat16 [4, 64, 256, 256], P('sec', 'tile')
- corrections: float32 [6, 4, 256], P(None, 'sec', 'tile')
Inputs may be any that keep to these rules, and one draw needn't show every extreme that they name: `owner`: in each section, the bands of one device's 4 tiles (aligned blocks of 64 rows) name no grid tile more than 2 times; in some blocks one grid tile is named exactly 2 times.
All inputs are finite; a program needn't handle non-finite values.
Results may differ from a plain program's by a relative error of at most 0.0018.
The roundings to bfloat16 on the way count: a program that leaves them out, or rounds other values in their place, can miss the bound.
Values may be sent and summed in bfloat16 or wider, within the bound.
A program may use at most 64 MiB of HBM per device.

v0:
```python
import math

import jax
import jax.numpy as jnp
from jax import lax
from jax.sharding import PartitionSpec as P

BAND = 16
ITERS = 2


COUPLING = 0.25


def passed_along(block, axis, distance):
    devices = range(lax.axis_size(axis))
    route = [(i - distance, i) for i in devices if i - distance in devices]
    return lax.ppermute(block, axis, route)


def padded_2(cells, sides, width):
    for axis, dim in sides:
        count = lax.axis_size(axis)
        ends = count - 1
        head = lax.slice_in_dim(cells, 0, width, axis=dim)
        tail = lax.slice_in_dim(cells, cells.shape[dim] - width, cells.shape[dim], axis=dim)
        cells = jnp.concatenate(
            [
                lax.ppermute(tail, axis, [(i, (i + 1) % count) for i in range(ends)]),
                cells,
                lax.ppermute(head, axis, [((i + 1) % count, i) for i in range(ends)]),
            ],
            axis=dim,
        )
    return cells


def hat_weight(distance):
    return jnp.maximum(0.0, 1.0 - jnp.abs(distance))


def sample_points(zoom, frac, offset, frame, source):
    scale = zoom * (frame / source)
    spots = jnp.arange(frame, dtype=jnp.float32)
    return (spots - offset.astype(jnp.float32)[..., None] - frac[..., None]) / scale[..., None]


def coverage(points, source):
    return jnp.clip(jnp.minimum(points + 1.0, source - points), 0.0, 1.0)


def moments(intensity, target, row_cover, col_cover, row_pos, frame):
    middle = (frame - 1) / 2.0
    level = intensity.astype(jnp.float32)
    error = target.astype(jnp.float32) - level
    weight = row_cover[:, :, None] * col_cover[:, None, :] / (frame * frame)
    columns = (jnp.arange(frame, dtype=jnp.float32) - middle) / (frame / 2.0)
    row_coord = (row_pos - middle) / (frame / 2.0)
    x_grid = jnp.broadcast_to(columns[None, None, :], level.shape)
    y_grid = jnp.broadcast_to(row_coord[:, :, None], level.shape)
    features = jnp.stack(
        [jnp.ones_like(level), x_grid, y_grid, level, level * x_grid, level * y_grid], axis=1
    )
    weighted = features * weight[:, None]
    normal = jnp.einsum("bfrq,bgrq->bfg", weighted, features, precision=lax.Precision.HIGHEST)
    gradient = jnp.einsum("bfrq,brq->bf", weighted, error, precision=lax.Precision.HIGHEST)
    return (normal, gradient)


def blocked_moments(intensity, target, row_cover, col_cover, row_pos, frame):
    count = intensity.shape[0]
    block_size = math.gcd(count, 64)

    def block_moments(block_args):
        return moments(
            block_args[0], block_args[1], block_args[2], block_args[3], block_args[4], frame
        )

    shaped = tuple(
        (
            member.reshape((count // block_size, block_size) + member.shape[1:])
            for member in (intensity, target, row_cover, col_cover, row_pos)
        )
    )
    normal, gradient = lax.map(block_moments, shaped)
    return (normal.reshape(count, 6, 6), gradient.reshape(count, 6))


def slot_table(routes, devices):
    matches = (routes[..., None] == jnp.arange(devices, dtype=jnp.int32)).astype(jnp.int32)
    before = jnp.cumsum(matches, axis=-2) - matches
    return jnp.sum(before * matches, axis=-1)


def precond_norm(residual, scaled):
    return lax.psum(jnp.sum(residual * scaled), ("sec", "tile"))


def shards(patches, zoom, frac, offset, owner, top_grid):
    sections, tile_count, source, _ = patches.shape
    frame = top_grid.shape[1]
    devices = lax.axis_size("tile")
    my_tile = lax.axis_index("tile")
    band_count = frame // BAND
    row_count = tile_count * band_count
    capacity = max(2, 2 * row_count // devices)
    slot_total = devices * capacity
    all_tiles = tile_count * devices
    points = sample_points(zoom, frac, offset, frame, source)
    covered = coverage(points, source)
    own_points = lax.dynamic_slice_in_dim(points, my_tile * tile_count, tile_count, 2)
    spots = jnp.arange(source, dtype=jnp.float32)
    weights = hat_weight(own_points[..., None] - spots).astype(jnp.bfloat16)
    halfway = jnp.einsum(
        "stqp,stpr->stqr", weights[:, 0], patches, preferred_element_type=jnp.float32
    ).astype(jnp.bfloat16)
    rendered = jnp.einsum(
        "stqr,stwr->stqw", halfway, weights[:, 1], preferred_element_type=jnp.float32
    ).astype(jnp.bfloat16)
    band_data = rendered.reshape(sections, row_count, BAND * frame)
    routes = owner[..., 0].reshape(sections, devices, row_count)
    slots = slot_table(routes, devices)
    own_routes = lax.dynamic_index_in_dim(routes, my_tile, 1, keepdims=False)
    own_slots = lax.dynamic_index_in_dim(slots, my_tile, 1, keepdims=False)
    positions = own_routes * capacity + own_slots
    slot_ids = jnp.arange(slot_total, dtype=jnp.int32)
    send_select = (positions[:, None, :] == slot_ids[None, :, None]).astype(jnp.bfloat16)
    outgoing = jnp.einsum(
        "smr,srx->smx", send_select, band_data, preferred_element_type=jnp.float32
    ).astype(jnp.bfloat16)
    incoming = lax.all_to_all(
        outgoing.reshape(sections, devices, capacity, BAND * frame),
        "tile",
        split_axis=1,
        concat_axis=1,
        tiled=True,
    )
    incoming = incoming.reshape(sections, slot_total, BAND * frame)
    is_mine = routes == my_tile
    cap_ids = jnp.arange(capacity, dtype=jnp.int32)
    receive_hit = (
        is_mine[:, :, None, :] & (slots[:, :, None, :] == cap_ids[None, None, :, None])
    ).astype(jnp.float32)
    receive_hit = receive_hit.reshape(sections, slot_total, row_count)
    band_of_row = jnp.arange(row_count, dtype=jnp.int32) % band_count
    band_onehot = (band_of_row[:, None] == jnp.arange(band_count, dtype=jnp.int32)[None, :]).astype(
        jnp.float32
    )
    tile_of_row = jnp.arange(row_count, dtype=jnp.int32) // band_count
    tile_onehot = (tile_of_row[:, None] == jnp.arange(tile_count, dtype=jnp.int32)[None, :]).astype(
        jnp.float32
    )
    slot_band = jnp.einsum("smr,rk->smk", receive_hit, band_onehot, precision=lax.Precision.HIGHEST)
    band_select = jnp.einsum(
        "smr,rk->skm", receive_hit, band_onehot, precision=lax.Precision.HIGHEST
    ).astype(jnp.bfloat16)
    image_sum = jnp.einsum(
        "skm,smx->skx", band_select, incoming, preferred_element_type=jnp.float32
    )
    own_share = (routes.reshape(sections, all_tiles, band_count) == my_tile).astype(jnp.float32)
    row_bands = covered[:, 0].reshape(sections, all_tiles, band_count, BAND)
    cover_sum = jnp.einsum(
        "sik,sikr,siw->skrw", own_share, row_bands, covered[:, 1], precision=lax.Precision.HIGHEST
    )
    grid_local = (image_sum.reshape(sections, band_count, BAND, frame) / (1.0 + cover_sum)).astype(
        jnp.bfloat16
    )
    grid_local = grid_local.reshape(sections, frame, frame)
    from_next = passed_along(grid_local[0], "sec", -1)
    at_top = lax.axis_index("sec") == lax.axis_size("sec") - 1
    boundary = jnp.where(at_top, top_grid[0], from_next)
    above = jnp.concatenate([grid_local[1:], boundary[None]], axis=0).reshape(
        sections, band_count, BAND * frame
    )
    slot_target = jnp.einsum(
        "smk,skx->smx", slot_band.astype(jnp.bfloat16), above, preferred_element_type=jnp.float32
    ).astype(jnp.bfloat16)
    band_spots = jnp.arange(BAND, dtype=jnp.float32)
    matches = receive_hit.reshape(sections, devices, capacity, row_count)
    source_rows = row_bands.reshape(sections, devices, row_count, BAND)
    slot_rows = jnp.einsum("sjcr,sjrb->sjcb", matches, source_rows, precision=lax.Precision.HIGHEST)
    source_cols = covered[:, 1].reshape(sections, devices, tile_count, frame)
    slot_cols = jnp.einsum(
        "sjcr,rt,sjtw->sjcw", matches, tile_onehot, source_cols, precision=lax.Precision.HIGHEST
    )
    band_index = jnp.einsum(
        "smk,k->sm",
        slot_band,
        jnp.arange(band_count, dtype=jnp.float32),
        precision=lax.Precision.HIGHEST,
    )
    row_pos = band_index[..., None] * BAND + band_spots
    normal, gradient = blocked_moments(
        incoming.reshape(-1, BAND, frame),
        slot_target.reshape(-1, BAND, frame),
        slot_rows.reshape(-1, BAND),
        slot_cols.reshape(-1, frame),
        row_pos.reshape(-1, BAND),
        frame,
    )
    normal_back, gradient_back = (
        lax.all_to_all(
            normal.reshape(sections, slot_total, 36),
            "tile",
            split_axis=1,
            concat_axis=1,
            tiled=True,
        ),
        lax.all_to_all(
            gradient.reshape(sections, slot_total, 6),
            "tile",
            split_axis=1,
            concat_axis=1,
            tiled=True,
        ),
    )
    tile_select = jnp.einsum(
        "smr,rt->smt", send_select.astype(jnp.float32), tile_onehot, precision=lax.Precision.HIGHEST
    )
    tile_normal = jnp.einsum(
        "smf,smt->stf", normal_back, tile_select, precision=lax.Precision.HIGHEST
    ).reshape(sections, tile_count, 6, 6)
    tile_gradient = jnp.einsum(
        "smf,smt->stf", gradient_back, tile_select, precision=lax.Precision.HIGHEST
    )
    right_side = jnp.transpose(tile_gradient, (2, 0, 1))
    diagonal_part = jnp.transpose(jnp.diagonal(tile_normal, axis1=2, axis2=3), (2, 0, 1))
    precond = 1.0 / (diagonal_part + 4.0 * COUPLING)
    solution = jnp.zeros_like(right_side)
    residual = right_side
    scaled = precond * residual
    direction = scaled
    current = precond_norm(residual, scaled)
    for step in range(ITERS):
        padded = padded_2(direction, (("sec", 1), ("tile", 2)), 1)
        beside = (
            padded[:, 2:, 1:-1] + padded[:, :-2, 1:-1] + padded[:, 1:-1, 2:] + padded[:, 1:-1, :-2]
        )
        image = jnp.einsum(
            "stfg,gst->fst", tile_normal, direction, precision=lax.Precision.HIGHEST
        ) + COUPLING * (4.0 * direction - beside)
        alpha = current / lax.psum(jnp.sum(direction * image), ("sec", "tile"))
        solution = solution + alpha * direction
        if step + 1 < ITERS:
            residual = residual - alpha * image
            scaled = precond * residual
            following = precond_norm(residual, scaled)
            direction = scaled + following / current * direction
            current = following
    return (grid_local[:, None], solution)


def solution(mesh):
    placed = (
        P("sec", "tile", None, None),
        P("sec", None, None),
        P("sec", None, None),
        P("sec", None, None),
        P("sec", None, None, None),
        P("tile", None, None),
    )
    return jax.shard_map(
        shards,
        mesh=mesh,
        in_specs=placed,
        out_specs=(P("sec", "tile", None, None), P(None, "sec", "tile")),
        check_vma=False,
    )
```

profile of v0, /device:TPU:1, one launch (start us, length us, event | category | flops | bytes accessed | tf_op | source)
XLA Modules:
  0.0 521.8 jit_solution(8778714224952125789)
XLA Ops:
  1.9 2.3 fusion.19
  5.5 1.8 minimum_clamp_fusion
  7.3 2.0 maximum_convert_fusion
  9.3 2.5 fusion.28
  13.7 1.5 convolution_convert_fusion.1
  15.1 1.5 reshape.414
  16.7 13.1 %all-to-all-start = ((bf16[1,64,2,4096]{3,2,0,1:T(2,128)(2,1)}), bf16[1,64,2,4096]{3,2,0,1:T(2,128)(2,1)S(1)}, u32[]{:S(2)}, u32[]{:S(2)}) async-start(bf16[1,64,2,4096]{3,2,0,1:T(2,128)(2,1)} %bitcast.182), calls=%async_computation | async-start | bytes 2097152 | tf_op jit(solution)/shard_map/all_to_all | solution.py:131
  29.9 1.8 fusion.73
  32.5 2.0 reshape.419
  41.9 1.7 broadcast_multiply_fusion.2
  43.5 2.7 fusion.75
  46.2 12.1 %all-to-all-done = bf16[1,64,2,4096]{3,2,0,1:T(2,128)(2,1)S(1)} async-done(((bf16[1,64,2,4096]{3,2,0,1:T(2,128)(2,1)}), bf16[1,64,2,4096]{3,2,0,1:T(2,128)(2,1)S(1)}, u32[]{:S(2)}, u32[]{:S(2)}) %all-to-all-start) | async-done | bytes 1048608 | tf_op jit(solution)/shard_map/all_to_all | solution.py:131
  59.5 2.3 copy.60
  61.8 1.6 fusion.74
  63.4 1.5 fusion.32
  67.1 1.5 reshape_reshape_reshape.3
  68.6 4.2 collective-permute-done
  75.6 154.9 %while.15 = (s32[]{:T(128)}, f32[2,64,6,6]{3,2,1,0:T(8,128)}, f32[2,64,6]{1,2,0:T(8,128)S(1)}, f32[2,64,16]{2,1,0:T(8,128)S(1)}, bf16[2,64,16,256]{3,2,1,0:T(8,1...) while((s32[]{:T(128)}, f32[2,64,6,6]{3,2,1,0:T(8,128)}, ...), condition=%wide.region_3.4_spmd, body=%wide.region_2.3_spmd.sunk | while | flops 137628160 | bytes 53981332 | solution.py:85
  76.9 3.3 broadcast_multiply_fusion.4
  80.2 1.8 fusion.109
  82.0 2.0 broadcast_in_dim.86
  84.0 2.0 broadcast_in_dim.85
  86.0 2.0 broadcast.447
  88.0 20.8 %stack.11 = f32[64,6,16,256]{3,1,2,0:T(8,128)} concatenate(f32[64,1,16,256]{3,1,2,0:T(1,128)} %broadcast.447, f32[64,1,16,256]{3,1,2,0:T(1,128)} %broadcast_in_dim.85, f32[64,1,16,256]{3,1,2,0:T(1,128)} %broadcast_in_dim.86, f32[64,1,16,256]{3,1,2,0:T(1,128)} %fusion.109, f32[64,1,16,256]{3,1,2,0:T(1,128)} %get-tuple-element.254, f32[64,1,16,256]{3,1,2,0:T(1,128)} %get-tuple-element.255), dimensions={1} | concatenate | bytes 12582912 | tf_op jit(solution)/shard_map/while/body/eval_jaxpr/stack | solution.py:61
  110.1 20.9 %fusion.111 = f32[64,1,6,1]{2,1,3,0:T(1,128)S(1)} fusion(f32[64,6,16,256]{3,1,2,0:T(8,128)} %stack.11, f32[64,16,256]{2,1,0:T(8,128)S(1)} %multiply_multiply_fusion.2, bf16[1,64,16,256]{3,2,1,0:T(8,128)(2,1)S(1)} %get-tuple-element.257, bf16[1,64,16,256]{3,2,1,0:T(8,128)(2,1)S(1)} %get-tuple-element.253), kind=kOutput, calls=%fused_computation.1.clone.1 | convolution fusion | flops 21233664 | bytes 8390144 | tf_op jit(solution)/shard_map/while/body/eval_jaxpr/bfrq,brq->bf/dot_general | solution.py:66
  131.0 22.0 %fusion.110 = f32[2,64,6,6]{3,2,1,0:T(8,128)} fusion(f32[2,64,6,6]{3,2,1,0:T(8,128)} %get-tuple-element.269, s32[]{:T(128)} %get-tuple-element.268, f32[64,6,16,256]{3,1,2,0:T(8,128)} %stack.11, f32[64,16,256]{2,1,0:T(8,128)} %copy-done.1), kind=kOutput, calls=%fused_computation.8.clone.1 | convolution fusion | flops 114819072 | bytes 18088448 | tf_op jit(solution)/shard_map/while/body/eval_jaxpr/bfrq,bgrq->bfg/dot_general | solution.py:65
  154.4 3.3 broadcast_multiply_fusion.4
  157.6 1.8 fusion.109
  159.4 2.0 broadcast_in_dim.86
  161.5 2.0 broadcast_in_dim.85
  163.5 2.0 broadcast.447
  165.5 20.8 %stack.11 = f32[64,6,16,256]{3,1,2,0:T(8,128)} concatenate(f32[64,1,16,256]{3,1,2,0:T(1,128)} %broadcast.447, f32[64,1,16,256]{3,1,2,0:T(1,128)} %broadcast_in_dim.85, f32[64,1,16,256]{3,1,2,0:T(1,128)} %broadcast_in_dim.86, f32[64,1,16,256]{3,1,2,0:T(1,128)} %fusion.109, f32[64,1,16,256]{3,1,2,0:T(1,128)} %get-tuple-element.254, f32[64,1,16,256]{3,1,2,0:T(1,128)} %get-tuple-element.255), dimensions={1} | concatenate | bytes 12582912 | tf_op jit(solution)/shard_map/while/body/eval_jaxpr/stack | solution.py:61
  187.5 20.9 %fusion.111 = f32[64,1,6,1]{2,1,3,0:T(1,128)S(1)} fusion(f32[64,6,16,256]{3,1,2,0:T(8,128)} %stack.11, f32[64,16,256]{2,1,0:T(8,128)S(1)} %multiply_multiply_fusion.2, bf16[1,64,16,256]{3,2,1,0:T(8,128)(2,1)S(1)} %get-tuple-element.257, bf16[1,64,16,256]{3,2,1,0:T(8,128)(2,1)S(1)} %get-tuple-element.253), kind=kOutput, calls=%fused_computation.1.clone.1 | convolution fusion | flops 21233664 | bytes 8390144 | tf_op jit(solution)/shard_map/while/body/eval_jaxpr/bfrq,brq->bf/dot_general | solution.py:66
  208.5 22.0 %fusion.110 = f32[2,64,6,6]{3,2,1,0:T(8,128)} fusion(f32[2,64,6,6]{3,2,1,0:T(8,128)} %get-tuple-element.269, s32[]{:T(128)} %get-tuple-element.268, f32[64,6,16,256]{3,1,2,0:T(8,128)} %stack.11, f32[64,16,256]{2,1,0:T(8,128)} %copy-done.1), kind=kOutput, calls=%fused_computation.8.clone.1 | convolution fusion | flops 114819072 | bytes 18088448 | tf_op jit(solution)/shard_map/while/body/eval_jaxpr/bfrq,bgrq->bfg/dot_general | solution.py:65
  230.5 1.8 reshape.455
  232.3 6.6 %all-to-all-start.2 = ((f32[1,128,36]{2,0,1:T(1,128)}), f32[1,128,36]{2,0,1:T(1,128)S(1)}, u32[]{:S(2)}, u32[]{:S(2)}) async-start(f32[1,128,36]{2,0,1:T(1,128)} %bitcast.62), calls=%async_computation.2 | async-start | bytes 131072 | tf_op jit(solution)/shard_map/all_to_all | solution.py:202
  239.6 9.0 %all-to-all-done.2 = f32[1,128,36]{2,0,1:T(1,128)S(1)} async-done(((f32[1,128,36]{2,0,1:T(1,128)}), f32[1,128,36]{2,0,1:T(1,128)S(1)}, u32[]{:S(2)}, u32[]{:S(2)}) %all-to-all-start.2) | async-done | bytes 18464 | tf_op jit(solution)/shard_map/all_to_all | solution.py:202
  248.6 4.4 all-to-all-start.1
  254.4 8.5 %all-to-all-done.1 = f32[1,128,6]{2,0,1:T(1,128)S(1)} async-done(((f32[1,128,6]{2,0,1:T(1,128)}), f32[1,128,6]{2,0,1:T(1,128)S(1)}, u32[]{:S(2)}, u32[]{:S(2)}) %all-to-all-start.1) | async-done | bytes 3104 | tf_op jit(solution)/shard_map/all_to_all | solution.py:209
  264.4 4.0 collective-permute-start.2
  269.1 3.4 collective-permute-start.3
  272.6 2.3 collective-permute-start.4
  276.3 76.8 %all-reduce = (f32[]{:T(128)}, f32[]{:T(128)}) all-reduce(f32[]{:T(128)} %get-tuple-element.161, f32[]{:T(128)} %get-tuple-element.160), channel_id=1, replica_groups=mesh['sec'=4,'tile'=64] {'sec','tile'}, use_global_device_ids=true, to_apply=%region_5.6 | all-reduce | flops 2 | bytes 16 | tf_op jit(solution)/shard_map/psum | solution.py:96
  355.0 74.0 %psum.30 = f32[]{:T(128)} all-reduce(f32[]{:T(128)} %multiply_reduce_fusion), channel_id=1, replica_groups=mesh['sec'=4,'tile'=64] {'sec','tile'}, use_global_device_ids=true, to_apply=%region_9.10 | all-reduce | flops 1 | bytes 8 | tf_op jit(solution)/shard_map/psum | solution.py:96
  431.5 4.0 collective-permute-start.6
  436.3 3.7 collective-permute-start.7
  440.0 2.8 collective-permute-start.8
  444.2 75.6 %psum.31 = f32[]{:T(128)} all-reduce(f32[]{:T(128)} %fusion.64), channel_id=1, replica_groups=mesh['sec'=4,'tile'=64] {'sec','tile'}, use_global_device_ids=true, to_apply=%region_11.12 | all-reduce | flops 1 | bytes 8 | tf_op jit(solution)/shard_map/psum | solution.py:242
  (110 shorter events, 34.1 us)
Async XLA Ops:
  0.6 8.7 %copy-start = (bf16[1,4,512,512]{3,2,1,0:T(8,128)(2,1)S(1)}, bf16[1,4,512,512]{3,2,1,0:T(8,128)(2,1)}, u32[]{:S(2)}) copy-start(bf16[1,4,512,512]{3,2,1,0:T(8,128)(2,1)} %param.8) | copy-start | bytes 6291460
  13.1 0.6 copy-start.6
  15.1 14.8 %copy-start.4 = (s32[1,256,16,1]{1,3,2,0:T(1,128)S(1)}, s32[1,256,16,1]{1,3,2,0:T(1,128)}, u32[]{:S(2)}) copy-start(s32[1,256,16,1]{1,3,2,0:T(1,128)} %param.12) | copy-start | bytes 49156
  16.7 41.7 %all-to-all-start = ((bf16[1,64,2,4096]{3,2,0,1:T(2,128)(2,1)}), bf16[1,64,2,4096]{3,2,0,1:T(2,128)(2,1)S(1)}, u32[]{:S(2)}, u32[]{:S(2)}) async-start(bf16[1,64,2,4096]{3,2,0,1:T(2,128)(2,1)} %bitcast.182), calls=%async_computation | async-start | bytes 2097152 | tf_op jit(solution)/shard_map/all_to_all | solution.py:131
  29.9 6.1 %copy-start.2 = (s32[64,64]{1,0:T(8,128)}, s32[64,64]{1,0:T(8,128)S(1)}, u32[]{:S(2)}) copy-start(s32[64,64]{1,0:T(8,128)S(1)} %copy.57) | copy-start | bytes 49156
  34.6 2.3 copy-start.8
  36.0 0.9 copy-start.3
  59.5 7.4 %copy-start.7 = (s32[64]{0:T(128)S(1)}, s32[64]{0:T(128)}, u32[]{:S(2)}) copy-start(s32[64]{0:T(128)} %copy-done.6) | copy-start | bytes 772
  59.5 7.4 %copy-start.9 = (s32[64]{0:T(128)S(1)}, s32[64]{0:T(128)}, u32[]{:S(2)}) copy-start(s32[64]{0:T(128)} %copy-done.8) | copy-start | bytes 772
  65.7 7.2 %collective-permute-start = (bf16[256,256]{1,0:T(8,128)(2,1)}, bf16[256,256]{1,0:T(8,128)(2,1)}, u32[]{:S(2)}, u32[]{:S(2)}) collective-permute-start(bf16[256,256]{1,0:T(8,128)(2,1)} %bitcast.31), channel_id=1, source_target_pairs={{64,0},{128,64},{192,128},{65,1},{129,65},{193,129},{66,2},{130,66... | collective-permute-start | bytes 393224 | tf_op jit(solution)/shard_map/ppermute | solution.py:18
  68.6 7.0 %copy-start.5 = (f32[2,64,6]{1,2,0:T(8,128)S(1)}, f32[2,64,6]{1,2,0:T(8,128)}, u32[]{:S(2)}) copy-start(f32[2,64,6]{1,2,0:T(8,128)} %custom-call.3) | copy-start | bytes 9220
  109.1 1.0 copy-start.1
  186.5 1.0 copy-start.1
  232.3 16.3 %all-to-all-start.2 = ((f32[1,128,36]{2,0,1:T(1,128)}), f32[1,128,36]{2,0,1:T(1,128)S(1)}, u32[]{:S(2)}, u32[]{:S(2)}) async-start(f32[1,128,36]{2,0,1:T(1,128)} %bitcast.62), calls=%async_computation.2 | async-start | bytes 131072 | tf_op jit(solution)/shard_map/all_to_all | solution.py:202
  248.6 14.3 %all-to-all-start.1 = ((f32[1,128,6]{2,0,1:T(1,128)}), f32[1,128,6]{2,0,1:T(1,128)S(1)}, u32[]{:S(2)}, u32[]{:S(2)}) async-start(f32[1,128,6]{2,0,1:T(1,128)} %bitcast.32), calls=%async_computation.1 | async-start | bytes 131072 | tf_op jit(solution)/shard_map/all_to_all | solution.py:209
  263.1 5.6 %collective-permute-start.1 = (f32[6,1,4]{0,2,1:T(4,128)S(1)}, f32[6,1,4]{0,2,1:T(4,128)S(1)}, u32[]{:S(2)}, u32[]{:S(2)}) collective-permute-start(f32[6,1,4]{0,2,1:T(4,128)S(1)} %get-tuple-element.195), channel_id=1, source_target_pairs={{64,0},{128,64},{192,128},{65,1},{129,65},{193,129},{66,2},{130,66... | collective-permute-start | bytes 296 | tf_op jit(solution)/shard_map/ppermute | solution.py:31
  264.4 4.7 collective-permute-start.2
  269.1 5.7 %collective-permute-start.3 = (f32[6,3,1]{0,2,1:T(1,128)S(1)}, f32[6,3,1]{0,2,1:T(1,128)S(1)}, u32[]{:S(2)}, u32[]{:S(2)}) collective-permute-start(f32[6,3,1]{0,2,1:T(1,128)S(1)} %get-tuple-element.191), channel_id=1, source_target_pairs={{1,0},{2,1},{3,2},{4,3},{5,4},{6,5},{7,6},{8,7},{9,8},{10,9},{11,1... | collective-permute-start | bytes 224 | tf_op jit(solution)/shard_map/ppermute | solution.py:31
  272.6 3.1 collective-permute-start.4
  430.2 5.5 %collective-permute-start.5 = (f32[6,1,4]{0,2,1:T(4,128)S(1)}, f32[6,1,4]{0,2,1:T(4,128)S(1)}, u32[]{:S(2)}, u32[]{:S(2)}) collective-permute-start(f32[6,1,4]{0,2,1:T(4,128)S(1)} %multiply_add_fusion.1), channel_id=1, source_target_pairs={{64,0},{128,64},{192,128},{65,1},{129,65},{193,129},{66,2},{130,66... | collective-permute-start | bytes 296 | tf_op jit(solution)/shard_map/ppermute | solution.py:31
  431.5 4.7 collective-permute-start.6
  436.3 6.5 %collective-permute-start.7 = (f32[6,3,1]{0,2,1:T(1,128)S(1)}, f32[6,3,1]{0,2,1:T(1,128)S(1)}, u32[]{:S(2)}, u32[]{:S(2)}) collective-permute-start(f32[6,3,1]{0,2,1:T(1,128)S(1)} %get-tuple-element.189), channel_id=1, source_target_pairs={{1,0},{2,1},{3,2},{4,3},{5,4},{6,5},{7,6},{8,7},{9,8},{10,9},{11,1... | collective-permute-start | bytes 224 | tf_op jit(solution)/shard_map/ppermute | solution.py:31
  440.0 3.5 collective-permute-start.8
where the time goes:
time: 528 us; the launch traced here: 522 us
  blocking collectives  226 us (43%)
  matrix products  99.2 us (19%)
  local copies, waits for them, and re-layouts  82.3 us (16%)
  starting transfers between devices  48.1 us (9%)
  waiting for transfers between devices  36.3 us (7%)
  other arithmetic  24.3 us (5%)
    psum x2, blocking collectives, precond_norm(): return lax.psum(jnp.sum(residual * scaled), ('sec', 'tile'))  151 us
    psum x1, blocking collectives, shards(): alpha = current / lax.psum(jnp.sum(direction * image), ('sec', 'tile'))  75.6 us
    dot_general x2, matrix products, moments(): jnp.einsum('bfrq,bgrq->bfg', weighted, features, precision=lax.Precision....  44 us
    dot_general x2, matrix products, moments(): jnp.einsum('bfrq,brq->bf', weighted, error, precision=lax.Precision.HIGHEST)  41.8 us
    another operation x2, local copies, waits for them, and re-layouts, moments(): jnp.stack([jnp.ones_like(level), x_grid, y_grid, level, level * x_grid, l...  41.7 us
    all_to_all x1, starting transfers between devices, shards(): lax.all_to_all(outgoing.reshape(sections, devices, capacity, BAND * frame...  13.1 us
    ppermute x4, starting transfers between devices, padded_2(): lax.ppermute(tail, axis, [(i, (i + 1) % count) for i in range(ends)])  13.1 us
    all_to_all x1, waiting for transfers between devices, shards(): lax.all_to_all(outgoing.reshape(sections, devices, capacity, BAND * frame...  12.1 us
  transfers between devices with their start and end apart: 12, of which 8 were waited for; matrix products, arithmetic and copies ran while one was open for 4% of the time, Pallas kernels for 0%

commit v1 on v0

v1 whole, which is shorter than its diff:
```python
import functools

import jax
import jax.numpy as jnp
from jax import lax
from jax.experimental import pallas as pl
from jax.experimental.pallas import tpu as pltpu
from jax.sharding import PartitionSpec as P

BAND = 16
ITERS = 2
COUPLING = 0.25
MESH = pl.DeviceIdType.MESH
F32 = jnp.float32
BF16 = jnp.bfloat16

MONOMIALS = ((0, 0), (1, 0), (0, 1), (2, 0), (1, 1), (0, 2))
PAIR = ((0, 1, 2), (1, 3, 4), (2, 4, 5))
GRADS = 6


def moment_of(f, g):
    return (f // 3 + g // 3) * 6 + PAIR[f % 3][g % 3]


def iota(shape, dim):
    return lax.broadcasted_iota(jnp.int32, shape, dim)


def fiota(shape, dim):
    return iota(shape, dim).astype(F32)


def shifted(x, distance):
    width = x.shape[1]
    return pltpu.roll(x, (-distance) % width, 1)


def total(x):
    return jnp.sum(jnp.sum(x, axis=0, keepdims=True), axis=1, keepdims=True)


def kernel(
    sections, devices, tiles, source, frame,
    zoom_hbm, frac_hbm, offset_hbm, routes_hbm, patch_hbm, top_hbm,
    grid_hbm, corr_ref,
    zoom_s, frac_s, offset_s, tab_s, tab_v, routes_v,
    patch_v, rendered, outgoing, incoming, weights, weights_hi, weights_lo, lit,
    select, grid_v, above, partial, values, returned, returning,
    payload, gathered_pair, chip_rows, gathered, planes,
    param_sem, route_sem, patch_sem, tab_sem, top_sem, out_sem,
    send_a, recv_a, send_g, recv_g, send_r, recv_r, send_p, recv_p, send_c, recv_c,
):
    bands = frame // BAND
    rows = tiles * bands
    me_sec = lax.axis_index("sec")
    me = lax.axis_index("tile")
    chip, core = me // 2, me % 2
    chips = devices // 2
    half = frame // 2
    middle = (frame - 1) / 2.0

    params = [
        pltpu.make_async_copy(a, b, param_sem.at[n])
        for n, (a, b) in enumerate(((zoom_hbm, zoom_s), (frac_hbm, frac_s), (offset_hbm, offset_s)))
    ]
    route_copy = pltpu.make_async_copy(routes_hbm, routes_v, route_sem)
    route_copy.start()
    for c in params:
        c.start()

    def patch_copy(t):
        return pltpu.make_async_copy(patch_hbm.at[t], patch_v.at[t], patch_sem.at[t])

    for t in range(tiles):
        patch_copy(t).start()
    top_copy = pltpu.make_async_copy(top_hbm, above, top_sem)

    @pl.when(me_sec == sections - 1)
    def _():
        top_copy.start()

    barrier = pltpu.get_barrier_semaphore()

    def greet(d, carry):
        pl.semaphore_signal(
            barrier, 1, device_id=(me_sec, lax.rem(me + d, devices)), device_id_type=MESH
        )
        return carry

    lax.fori_loop(1, devices, greet, 0)
    pair_peers = [
        (lax.rem(me_sec + ds, sections), chip * 2 + lax.rem(core + dc, 2))
        for ds in range(sections)
        for dc in range(2)
        if ds or dc
    ]
    for n, peer in enumerate(pair_peers):
        if n:
            pl.semaphore_signal(barrier, 1, device_id=peer, device_id_type=MESH)

    route_copy.wait()
    lane = iota((devices, 128), 1)
    mine = (routes_v[...] == me) & (lane < rows)
    take0 = jnp.min(jnp.where(mine, lane, rows - 1), axis=1, keepdims=True)
    take1 = jnp.max(jnp.where(mine, lane, 0), axis=1, keepdims=True)
    count = jnp.sum(jnp.where(mine, 1, 0), axis=1, keepdims=True)
    own_row = routes_v[pl.ds(me, 1), :]
    hit = (own_row == iota((devices, 128), 0)) & (lane < rows)
    out0 = jnp.min(jnp.where(hit, lane, rows - 1), axis=1, keepdims=True)
    out1 = jnp.max(jnp.where(hit, lane, 0), axis=1, keepdims=True)
    valid0 = count > 0
    valid1 = count > 1
    idx0, idx1 = take0, take1
    on0 = valid0.astype(jnp.int32)
    on1 = valid1.astype(jnp.int32)
    table = jnp.where(lane == 0, idx0, 0)
    table = jnp.where(lane == 1, idx1, table)
    table = jnp.where(lane == 2, out0, table)
    table = jnp.where(lane == 3, out1, table)
    table = jnp.where(lane == 4, on0, table)
    table = jnp.where(lane == 5, on1, table)
    tab_v[...] = table
    tab_copy = pltpu.make_async_copy(tab_v, tab_s, tab_sem)
    tab_copy.start()
    for c in params:
        c.wait()

    def scale_of(a, i):
        return zoom_s[a, i] * (frame / source)

    def points_of(spots, a, i):
        return (spots - offset_s[a, i].astype(F32) - frac_s[a, i]) / scale_of(a, i)

    def cover_of(points):
        return jnp.clip(jnp.minimum(points + 1.0, source - points), 0.0, 1.0)

    def hat(distance):
        return jnp.maximum(0.0, 1.0 - jnp.abs(distance)).astype(BF16)

    def render(t, carry):
        i = me * tiles + t
        down = points_of(fiota((frame, 128), 0), 0, i)
        down = jnp.concatenate([down] * (source // 128), axis=1)
        row_weights = hat(down - fiota((frame, source), 1))
        across = points_of(fiota((8, frame), 1), 1, i)
        across = jnp.broadcast_to(across[0:1], (source, frame))
        col_weights = hat(across - fiota((source, frame), 0))
        patch_copy(t).wait()
        halfway = jnp.dot(row_weights, patch_v[t], preferred_element_type=F32).astype(BF16)
        image = jnp.dot(halfway, col_weights, preferred_element_type=F32).astype(BF16)
        rendered[pl.ds(pl.multiple_of(t * bands, bands), bands)] = image.reshape(bands, BAND, frame)
        return carry

    lax.fori_loop(0, tiles, render, 0)

    tab_copy.wait()

    def pack(g, carry):
        outgoing[g, 0] = rendered[tab_s[g, 2] & (rows - 1)]
        outgoing[g, 1] = rendered[tab_s[g, 3] & (rows - 1)]
        return carry

    lax.fori_loop(0, devices, pack, 0)
    incoming[me] = outgoing[me]
    greeted = devices - 1 + len(pair_peers) - 1
    pl.semaphore_wait(barrier, greeted)

    def band_copy(peer, from_):
        return pltpu.make_async_remote_copy(
            src_ref=outgoing.at[peer],
            dst_ref=incoming.at[from_],
            send_sem=send_a.at[peer],
            recv_sem=recv_a.at[from_],
            device_id=(me_sec, peer),
            device_id_type=MESH,
        )

    def send_bands(d, carry):
        band_copy(lax.rem(me + d, devices), me).start()
        return carry

    lax.fori_loop(1, devices, send_bands, 0)

    def cover_slot(j, carry):
        for c in range(2):
            idx = tab_s[j, c] & (rows - 1)
            i = j * tiles + (idx >> 4)
            k = idx & (bands - 1)
            start = (k * BAND).astype(F32)
            down = cover_of(points_of(fiota((BAND, 128), 0) + start, 0, i))
            down = down * (tab_s[j, 4 + c].astype(F32) / (frame * frame))
            across = cover_of(points_of(fiota((8, frame), 1), 1, i))
            weight = jnp.concatenate([down, down], axis=1) * jnp.broadcast_to(
                across[0:1], (BAND, frame)
            )
            weights[j, c] = weight
            hi = weight.astype(BF16)
            weights_hi[j, c] = hi
            weights_lo[j, c] = (weight - hi.astype(F32)).astype(BF16)
        return carry

    lax.fori_loop(0, devices, cover_slot, 0)

    sub = iota((devices, 128), 0)
    band0 = jnp.where(valid0, (idx0 & (bands - 1)).astype(F32), -float(bands))
    band1 = jnp.where(valid1, (idx1 & (bands - 1)).astype(F32), -float(bands))
    along = jnp.where(lane == sub, band0, 0.0) + jnp.where(lane == sub + devices, band1, 0.0)
    along = jnp.broadcast_to(jnp.sum(along, axis=0, keepdims=True), (8, 128)).astype(BF16)
    chunk = 256 // (2 * BAND)
    chunks = devices // chunk
    wide = iota((128, 256), 1)

    def choose(h, cover):
        spread = (iota((128, 256), 0) == h * chunk + wide // (2 * BAND) + devices * ((wide // BAND) % 2))
        spread = jnp.where(spread, 1.0, 0.0).astype(BF16)
        target = jnp.dot(along, spread, preferred_element_type=F32)[0:1]
        target = target * BAND + (iota((1, 256), 1) % BAND).astype(F32)
        onehot = jnp.where(fiota((frame, 256), 0) == target, 1.0, 0.0).astype(BF16)
        select[h] = onehot
        at = pl.ds(pl.multiple_of(h * chunk, chunk), chunk)
        cover += jnp.dot(onehot, weights_hi[at].reshape(256, frame), preferred_element_type=F32)
        cover += jnp.dot(onehot, weights_lo[at].reshape(256, frame), preferred_element_type=F32)
        return cover

    cover = lax.fori_loop(0, chunks, choose, jnp.zeros((frame, frame), F32))
    cover = 1.0 + cover * float(frame * frame)

    row_lane = iota((1, 128), 1)

    def moments(t, payload):
        i = me * tiles + t
        down = cover_of(points_of(fiota((frame, 128), 0), 0, i)) / (frame * frame)
        y = (fiota((frame, 128), 0) - middle) / (frame / 2.0)
        down = [jnp.concatenate([v, v], axis=1) for v in (down, down * y, down * y * y)]
        across = cover_of(points_of(fiota((8, frame), 1), 1, i))[0:1]
        x = (fiota((1, frame), 1) - middle) / (frame / 2.0)
        across = (across, across * x, across * x * x)
        at = pl.ds(pl.multiple_of(t * bands, bands), bands)
        level = rendered[at].reshape(frame, frame).astype(F32)
        for p, image in enumerate((None, level, level * level)):
            for b in range(3):
                column = down[b] if image is None else down[b] * image
                column = jnp.sum(column, axis=0, keepdims=True)
                for m, (a, b2) in enumerate(MONOMIALS):
                    if b2 == b:
                        value = jnp.sum(column * across[a], axis=1, keepdims=True)
                        payload = jnp.where(
                            row_lane == GRADS * tiles + (p * 6 + m) * tiles + t, value, payload
                        )
                        if p >= 1 and (a + b) <= 1:
                            payload = jnp.where(
                                row_lane == ((p - 1) * 3 + m) * tiles + t, -value, payload
                            )
        return payload

    own = lax.fori_loop(0, tiles, moments, jnp.zeros((1, 128), F32))

    grid = jnp.zeros((frame, frame), F32)

    def arrive(h, grid):
        def one(n, carry):
            j = h * chunk + n

            @pl.when(j != me)
            def _():
                band_copy(j, j).wait_recv()

            return carry

        lax.fori_loop(0, chunk, one, 0)
        at = pl.ds(pl.multiple_of(h * chunk, chunk), chunk)
        return grid + jnp.dot(
            select[h], incoming[at].reshape(256, frame), preferred_element_type=F32
        )

    grid = lax.fori_loop(0, chunks, arrive, grid)
    grid_v[...] = (grid / cover).astype(BF16).reshape(bands, BAND, frame)
    write_grid = pltpu.make_async_copy(grid_v, grid_hbm, out_sem)
    write_grid.start()
    to_below = pltpu.make_async_remote_copy(
        src_ref=grid_v,
        dst_ref=above,
        send_sem=send_g,
        recv_sem=recv_g,
        device_id=(lax.rem(me_sec + sections - 1, sections), me),
        device_id_type=MESH,
    )

    @pl.when(me_sec > 0)
    def _():
        to_below.start()

    def weigh(j, carry):
        for c in range(2):
            lit[j, c] = weights[j, c] * incoming[j, c].astype(F32)
        return carry

    lax.fori_loop(0, devices, weigh, 0)

    @pl.when(me_sec < sections - 1)
    def _():
        to_below.wait_recv()

    @pl.when(me_sec == sections - 1)
    def _():
        top_copy.wait()

    x = (fiota((8, frame), 1) - middle) / (frame / 2.0)
    x0, x1 = x[:, :half], x[:, half:]
    y_base = (fiota((BAND, half), 0) - middle) / (frame / 2.0)

    def contract(j, carry):
        for c in range(2):
            k = tab_s[j, c] & (bands - 1)
            target = above[k].astype(F32)
            y = y_base + (k * BAND).astype(F32) / (frame / 2.0)
            for n, factor in enumerate((weights, lit)):
                product = target * factor[j, c]
                left, right = product[:, :half], product[:, half:]
                both = left + right
                left, right = left[:8] + left[8:], right[:8] + right[8:]
                y_part = both * y
                partial[c, n * 3, j] = left + right
                partial[c, n * 3 + 1, j] = left * x0 + right * x1
                partial[c, n * 3 + 2, j] = y_part[:8] + y_part[8:]
        return carry

    lax.fori_loop(0, devices, contract, 0)
    answer = jnp.zeros((devices, 128), F32)
    for c, (idx, valid) in enumerate(((idx0, valid0), (idx1, valid1))):
        tile_of = jnp.where(valid, idx // bands, -1)
        for f in range(GRADS):
            value = jnp.sum(jnp.sum(partial[c, f], axis=1), axis=1, keepdims=True)
            answer = answer + jnp.where(lane == f * tiles + tile_of, value, 0.0)
    values[...] = answer

    def unfold(j, carry):
        returned[j] = values[pl.ds(j, 1), :]
        return carry

    lax.fori_loop(0, devices, unfold, 0)
    returning[me] = returned[me]

    def sum_copy(peer, from_):
        return pltpu.make_async_remote_copy(
            src_ref=returned.at[peer],
            dst_ref=returning.at[from_],
            send_sem=send_r.at[peer],
            recv_sem=recv_r.at[from_],
            device_id=(me_sec, peer),
            device_id_type=MESH,
        )

    def send_sums(d, carry):
        sum_copy(lax.rem(me + d, devices), me).start()
        return carry

    lax.fori_loop(1, devices, send_sums, 0)

    def await_sums(d, carry):
        j = lax.rem(me + d, devices)
        sum_copy(j, j).wait_recv()
        return carry

    lax.fori_loop(1, devices, await_sums, 0)
    own = own + jnp.sum(returning[...], axis=0)

    payload[...] = own
    place = me_sec * 2 + core
    gathered_pair[place] = own

    def pair_copy(n, peer, from_):
        return pltpu.make_async_remote_copy(
            src_ref=payload,
            dst_ref=gathered_pair.at[from_],
            send_sem=send_p.at[n],
            recv_sem=recv_p.at[from_],
            device_id=peer,
            device_id_type=MESH,
        )

    for n, peer in enumerate(pair_peers):
        pair_copy(n, peer, place).start()
    for n, peer in enumerate(pair_peers):
        pair_copy(n, peer, peer[0] * 2 + lax.rem(peer[1], 2)).wait_recv()
    for n in range(2 * sections):
        chip_rows[n : n + 1, :] = gathered_pair[n]
    gathered[chip] = chip_rows[...]

    def chip_copy(other, from_):
        return pltpu.make_async_remote_copy(
            src_ref=chip_rows,
            dst_ref=gathered.at[from_],
            send_sem=send_c.at[other],
            recv_sem=recv_c.at[from_],
            device_id=(me_sec, other * 2 + core),
            device_id_type=MESH,
        )

    def send_rows(d, carry):
        chip_copy(lax.rem(chip + d, chips), chip).start()
        return carry

    lax.fori_loop(1, chips, send_rows, 0)

    def await_rows(d, carry):
        j = lax.rem(chip + d, chips)
        chip_copy(j, j).wait_recv()
        return carry

    lax.fori_loop(1, chips, await_rows, 0)
    everyone = 2 * sections * chips
    planes[...] = jnp.transpose(gathered[...].reshape(everyone, 128))

    shape = (8, everyone)
    lane_id = iota(shape, 1)
    tile_id = iota(shape, 0)
    pairs = 2 * sections
    lane_chip, lane_sec, lane_core = lane_id // pairs, (lane_id % pairs) // 2, lane_id % 2
    used = tile_id < tiles
    right_side = [
        jnp.where(used, planes[f * tiles : f * tiles + 8, :], 0.0) for f in range(GRADS)
    ]
    moment = [
        planes[(GRADS + m) * tiles : (GRADS + m) * tiles + 8, :] for m in range(18)
    ]
    precond = [
        jnp.where(used, 1.0 / (moment[moment_of(f, f)] + 4.0 * COUPLING), 0.0) for f in range(GRADS)
    ]
    has_next = ~((lane_chip == chips - 1) & (lane_core == 1)) | (tile_id < tiles - 1)
    has_before = ~((lane_chip == 0) & (lane_core == 0)) | (tile_id > 0)

    def beside_of(d):
        up = pltpu.roll(d, 7, 0)
        over = pltpu.roll(d, tiles - 1, 0)
        over = jnp.where(lane_core == 0, shifted(over, 1), shifted(over, pairs - 1))
        after = jnp.where(used & has_next, jnp.where(tile_id == tiles - 1, over, up), 0.0)
        down = pltpu.roll(d, 1, 0)
        under = pltpu.roll(d, 8 - (tiles - 1), 0)
        under = jnp.where(lane_core == 1, shifted(under, -1), shifted(under, 1 - pairs))
        before = jnp.where(used & has_before, jnp.where(tile_id == 0, under, down), 0.0)
        upper = jnp.where(lane_sec < sections - 1, shifted(d, 2), 0.0)
        lower = jnp.where(lane_sec > 0, shifted(d, -2), 0.0)
        return upper + lower + after + before

    def inner(left, right):
        return total(sum(a * b for a, b in zip(left, right)))

    residual = right_side
    scaled = [p * r for p, r in zip(precond, residual)]
    direction = scaled
    current = inner(residual, scaled)
    result = [jnp.zeros(shape, F32)] * GRADS
    for step in range(ITERS):
        image = [
            sum(moment[moment_of(f, g)] * direction[g] for g in range(GRADS))
            + COUPLING * (4.0 * direction[f] - beside_of(direction[f]))
            for f in range(GRADS)
        ]
        alpha = current / inner(direction, image)
        result = [c + alpha * d for c, d in zip(result, direction)]
        if step + 1 < ITERS:
            residual = [r - alpha * h for r, h in zip(residual, image)]
            scaled = [p * r for p, r in zip(precond, residual)]
            following = inner(residual, scaled)
            ratio = following / current
            direction = [z + ratio * d for z, d in zip(scaled, direction)]
            current = following
    my_lane = chip * pairs + place
    for f in range(GRADS):
        column = jnp.sum(jnp.where(lane_id == my_lane, result[f], 0.0), axis=1, keepdims=True)
        turned = jnp.where(iota((8, 128), 0) == iota((8, 128), 1), column, 0.0)
        corr_ref[f] = jnp.sum(turned, axis=0, keepdims=True)[:, :tiles]

    def sent(d, carry):
        peer = lax.rem(me + d, devices)
        band_copy(peer, me).wait_send()
        sum_copy(peer, me).wait_send()
        return carry

    lax.fori_loop(1, devices, sent, 0)

    def sent_rows(d, carry):
        chip_copy(lax.rem(chip + d, chips), chip).wait_send()
        return carry

    lax.fori_loop(1, chips, sent_rows, 0)
    for n, peer in enumerate(pair_peers):
        pair_copy(n, peer, place).wait_send()

    @pl.when(me_sec > 0)
    def _():
        to_below.wait_send()

    write_grid.wait()


def shards(patches, zoom, frac, offset, owner, top_grid):
    _, tiles, source, _ = patches.shape
    frame = top_grid.shape[1]
    sections, devices = lax.axis_size("sec"), lax.axis_size("tile")
    bands = frame // BAND
    rows = tiles * bands
    chips = devices // 2
    pairs = 2 * sections
    routes = jnp.pad(owner.reshape(devices, rows), ((0, 0), (0, 128 - rows)))
    any_space = pl.BlockSpec(memory_space=pl.ANY)
    vmem, smem, sem = pltpu.VMEM, pltpu.SMEM, pltpu.SemaphoreType.DMA
    all_tiles = tiles * devices
    grid, corrections = pl.pallas_call(
        functools.partial(kernel, sections, devices, tiles, source, frame),
        out_shape=(
            jax.ShapeDtypeStruct((bands, BAND, frame), BF16),
            jax.ShapeDtypeStruct((GRADS, 1, tiles), F32),
        ),
        in_specs=[any_space] * 6,
        out_specs=(any_space, pl.BlockSpec(memory_space=pltpu.VMEM)),
        scratch_shapes=[
            smem((2, all_tiles), F32),
            smem((2, all_tiles), F32),
            smem((2, all_tiles), jnp.int32),
            smem((devices, 128), jnp.int32),
            vmem((devices, 128), jnp.int32),
            vmem((devices, 128), jnp.int32),
            vmem((tiles, source, source), BF16),
            vmem((rows, BAND, frame), BF16),
            vmem((devices, 2, BAND, frame), BF16),
            vmem((devices, 2, BAND, frame), BF16),
            vmem((devices, 2, BAND, frame), F32),
            vmem((devices, 2, BAND, frame), BF16),
            vmem((devices, 2, BAND, frame), BF16),
            vmem((devices, 2, BAND, frame), F32),
            vmem((devices * 2 * BAND // 256, frame, 256), BF16),
            vmem((bands, BAND, frame), BF16),
            vmem((bands, BAND, frame), BF16),
            vmem((2, GRADS, devices, 8, 128), F32),
            vmem((devices, 128), F32),
            vmem((devices, 1, 128), F32),
            vmem((devices, 1, 128), F32),
            vmem((1, 128), F32),
            vmem((pairs, 1, 128), F32),
            vmem((pairs, 128), F32),
            vmem((chips, pairs, 128), F32),
            vmem((128, chips * pairs), F32),
            sem((3,)),
            sem,
            sem((tiles,)),
            sem,
            sem,
            sem,
            sem((devices,)),
            sem((devices,)),
            sem,
            sem,
            sem((devices,)),
            sem((devices,)),
            sem((pairs,)),
            sem((pairs,)),
            sem((chips,)),
            sem((chips,)),
        ],
        compiler_params=pltpu.CompilerParams(
            collective_id=0, has_side_effects=True, vmem_limit_bytes=48 << 20
        ),
    )(
        zoom[0],
        frac[0],
        offset[0],
        routes,
        patches[0],
        top_grid.reshape(bands, BAND, frame),
    )
    return (grid.reshape(1, 1, frame, frame), corrections)


def solution(mesh):
    placed = (
        P("sec", "tile", None, None),
        P("sec", None, None),
        P("sec", None, None),
        P("sec", None, None),
        P("sec", None, None, None),
        P("tile", None, None),
    )
    return jax.shard_map(
        shards,
        mesh=mesh,
        in_specs=placed,
        out_specs=(P("sec", "tile", None, None), P(None, "sec", "tile")),
        check_vma=False,
    )
```

time: 528 us -> 75.7 us (0.14); the launches traced: 522 us -> 75.4 us
  blocking collectives: 226 us -> 0 us
  matrix products: 99.2 us -> 0 us
  local copies, waits for them, and re-layouts: 82.3 us -> 6.76 us
  Pallas kernels: 0 us -> 68 us
  starting transfers between devices: 48.1 us -> 0 us
  waiting for transfers between devices: 36.3 us -> 0 us
  other arithmetic: 24.3 us -> 0 us
    psum x3 -> x0, blocking collectives: 226 us -> none  [the longest x2 151 us: precond_norm(): return lax.psum(jnp.sum(residual * scaled), ('sec', 'tile'))]
    dot_general x20 -> x0, matrix products: 99.2 us -> none  [the longest x2 44 us: moments(): jnp.einsum('bfrq,bgrq->bfg', weighted, features, precision=lax.Precision....]
    pallas_call x0 -> x1, Pallas kernels: none -> 68 us  [shards(): pl.pallas_call(functools.partial(kernel, sections, devices, tiles, source...]
    another operation x18 -> x0, local copies, waits for them, and re-layouts: 57.9 us -> none  [the longest x2 41.7 us: moments(): jnp.stack([jnp.ones_like(level), x_grid, y_grid, level, level * x_grid, l...]
    all_to_all x3 -> x0, waiting for transfers between devices: 29.6 us -> none  [the longest x1 12.1 us: shards(): lax.all_to_all(outgoing.reshape(sections, devices, capacity, BAND * frame...]
    all_to_all x3 -> x0, starting transfers between devices: 24.1 us -> none  [the longest x1 13.1 us: shards(): lax.all_to_all(outgoing.reshape(sections, devices, capacity, BAND * frame...]
    ppermute x9 -> x0, starting transfers between devices: 24 us -> none  [the longest x4 13.1 us: padded_2(): lax.ppermute(tail, axis, [(i, (i + 1) % count) for i in range(ends)])]
    broadcast_in_dim x4 -> x0, local copies, waits for them, and re-layouts: 8.09 us -> none  [moments(): jnp.stack([jnp.ones_like(level), x_grid, y_grid, level, level * x_grid, l...]
  transfers between devices with their start and end apart: 12 -> 0, of which waited for: 8 -> 0; matrix products, arithmetic and copies ran while one was open for 4% -> 0% of each run, Pallas kernels for 0% -> 0%
where the time goes in v1:
time: 75.7 us; the launch traced here: 75.4 us
  Pallas kernels  68 us (90%)
  local copies, waits for them, and re-layouts  6.76 us (9%)
    pallas_call x1, Pallas kernels, shards(): pl.pallas_call(functools.partial(kernel, sections, devices, tiles, source...  68 us
    unnamed x13, local copies, waits for them, and re-layouts  6.67 us

profile of v1, /device:TPU:1, one launch (start us, length us, event | category | flops | bytes accessed | tf_op | source)
XLA Modules:
  0.0 75.4 jit_solution(16741895084280019761)
XLA Ops:
  0.6 0.8 %copy.10 = s32[1,256,16,1]{2,1,3,0:T(8,128)S(1)} copy(s32[1,256,16,1]{1,3,2,0:T(1,128)} %param.10) | data formatting | bytes 32768 | tf_op args[4]
  1.4 0.1 reshape.13
  1.6 0.0 copy-start
  1.6 1.6 %copy-done = bf16[1,4,512,512]{3,2,1,0:T(8,128)(2,1)S(1)} copy-done((bf16[1,4,512,512]{3,2,1,0:T(8,128)(2,1)S(1)}, bf16[1,4,512,512]{3,2,1,0:T(8,128)(2,1)}, u32[]{:S(2)}) %copy-start) | copy-done | bytes 2097176
  3.2 0.0 copy-start.1
  3.2 0.9 %copy-done.1 = bf16[1,256,256]{2,1,0:T(8,128)(2,1)S(1)} copy-done((bf16[1,256,256]{2,1,0:T(8,128)(2,1)S(1)}, bf16[1,256,256]{2,1,0:T(8,128)(2,1)}, u32[]{:S(2)}) %copy-start.1) | copy-done | bytes 131096
  4.1 0.0 copy-start.2
  4.1 0.7 copy-done.2
  4.7 0.0 copy-start.3
  4.7 0.7 copy-done.3
  5.4 0.0 copy-start.4
  5.4 0.7 copy-done.4
  6.1 68.0 %shard_map.77 = (bf16[16,16,256]{2,1,0:T(8,128)(2,1)S(1)}, f32[6,1,4]{2,1,0:T(1,128)S(1)}) custom-call(f32[2,256]{1,0:T(2,128)S(1)} %bitcast.13, f32[2,256]{1,0:T(2,128)S(1)} %bitcast.14, s32[2,256]{1,0:T(2,128)S(1)} %bitcast.15, s32[64,128]{1,0:T(8,128)S(1)} %pad.4.routes_hbm, bf16[4,512,512]{2,1,0:T(8,128)(2,1)S(1)} %bitcast.10, ...), custom_call_target="tpu_custom_call" | custom-call | tf_op jit(solution)/shard_map/pallas_call | solution.py:511
  74.1 0.7 copy.11
  74.8 0.7 copy.13
  (1 shorter events, 0.0 us)
Async XLA Ops:
  1.6 1.6 %copy-start = (bf16[1,4,512,512]{3,2,1,0:T(8,128)(2,1)S(1)}, bf16[1,4,512,512]{3,2,1,0:T(8,128)(2,1)}, u32[]{:S(2)}) copy-start(bf16[1,4,512,512]{3,2,1,0:T(8,128)(2,1)} %param.6) | copy-start | bytes 6291460
  3.2 0.9 %copy-start.1 = (bf16[1,256,256]{2,1,0:T(8,128)(2,1)S(1)}, bf16[1,256,256]{2,1,0:T(8,128)(2,1)}, u32[]{:S(2)}) copy-start(bf16[1,256,256]{2,1,0:T(8,128)(2,1)} %param.11) | copy-start | bytes 393220
  4.1 0.7 copy-start.2
  4.7 0.7 copy-start.3
  5.4 0.7 copy-start.4

commit v2 on v1

--- a/solution.py
+++ b/solution.py
@@ -46,10 +46,10 @@
     grid_hbm, corr_ref,
     zoom_s, frac_s, offset_s, tab_s, tab_v, routes_v,
     patch_v, rendered, outgoing, incoming, weights, weights_hi, weights_lo, lit,
-    select, grid_v, above, partial, values, returned, returning,
-    payload, gathered_pair, chip_rows, gathered, planes,
+    select, grid_v, above, partial, home, mine_sums, all_sums, pair_sums, all_pairs, right_v,
+    mom_row, mom_rows, mom_turned, mom_mine, mom_all,
     param_sem, route_sem, patch_sem, tab_sem, top_sem, out_sem,
-    send_a, recv_a, send_g, recv_g, send_r, recv_r, send_p, recv_p, send_c, recv_c,
+    send_a, recv_a, send_g, recv_g, send_m, recv_m, send_x, recv_x, send_p, recv_p, send_c, recv_c,
 ):
     bands = frame // BAND
     rows = tiles * bands
@@ -226,6 +226,22 @@
     cover = lax.fori_loop(0, chunks, choose, jnp.zeros((frame, frame), F32))
     cover = 1.0 + cover * float(frame * frame)
 
+    def locate(n, carry):
+        first, second = carry
+        theirs = (routes_v[...] == 2 * n + core) & (lane < rows)
+        low = jnp.min(jnp.where(theirs, lane, rows - 1), axis=1, keepdims=True)
+        high = jnp.max(jnp.where(theirs, lane, 0), axis=1, keepdims=True)
+        named = jnp.sum(jnp.where(theirs, 1, 0), axis=1, keepdims=True)
+        low = jnp.where(named > 0, low >> 4, -1)
+        high = jnp.where(named > 1, high >> 4, -1)
+        return jnp.where(lane == n, low, first), jnp.where(lane == n, high, second)
+
+    nowhere = jnp.zeros((devices, 128), jnp.int32)
+    first, second = lax.fori_loop(0, chips, locate, (nowhere, nowhere))
+    where = jnp.transpose(jnp.concatenate([first, second], axis=0).astype(F32))
+    for n in range(chips):
+        home[n] = jnp.broadcast_to(where[n : n + 1], (8, 128))
+
     row_lane = iota((1, 128), 1)
 
     def moments(t, payload):
@@ -246,15 +262,29 @@
                     if b2 == b:
                         value = jnp.sum(column * across[a], axis=1, keepdims=True)
                         payload = jnp.where(
-                            row_lane == GRADS * tiles + (p * 6 + m) * tiles + t, value, payload
+                            row_lane == (p * 6 + m) * tiles + t, value, payload
                         )
-                        if p >= 1 and (a + b) <= 1:
-                            payload = jnp.where(
-                                row_lane == ((p - 1) * 3 + m) * tiles + t, -value, payload
-                            )
         return payload
 
     own = lax.fori_loop(0, tiles, moments, jnp.zeros((1, 128), F32))
+    mom_row[...] = own
+    mom_rows[me] = own
+
+    def moment_copy(peer, from_):
+        return pltpu.make_async_remote_copy(
+            src_ref=mom_row,
+            dst_ref=mom_rows.at[from_],
+            send_sem=send_m.at[peer],
+            recv_sem=recv_m.at[from_],
+            device_id=(me_sec, peer),
+            device_id_type=MESH,
+        )
+
+    def send_moments(d, carry):
+        moment_copy(lax.rem(me + d, devices), me).start()
+        return carry
+
+    lax.fori_loop(1, devices, send_moments, 0)
 
     grid = jnp.zeros((frame, frame), F32)
 
@@ -297,6 +327,32 @@
         return carry
 
     lax.fori_loop(0, devices, weigh, 0)
+
+    def await_moments(d, carry):
+        j = lax.rem(me + d, devices)
+        moment_copy(j, j).wait_recv()
+        return carry
+
+    lax.fori_loop(1, devices, await_moments, 0)
+    turned = jnp.concatenate([mom_rows[:, 0, :], jnp.zeros((devices, 128), F32)], axis=0)
+    mom_turned[...] = jnp.transpose(turned)
+    for h in range(2):
+        even, odd = (mom_turned[pl.ds(2 * h + n, 24, stride=tiles), :] for n in range(2))
+        mom_mine[h] = even + pltpu.roll(odd, devices, 1)
+    mom_all[me_sec] = mom_mine[...]
+
+    def section_copy(ds, from_):
+        return pltpu.make_async_remote_copy(
+            src_ref=mom_mine,
+            dst_ref=mom_all.at[from_],
+            send_sem=send_x.at[ds],
+            recv_sem=recv_x.at[from_],
+            device_id=(lax.rem(me_sec + ds, sections), me),
+            device_id_type=MESH,
+        )
+
+    for ds in range(1, sections):
+        section_copy(ds, me_sec).start()
 
     @pl.when(me_sec < sections - 1)
     def _():
@@ -327,53 +383,54 @@
         return carry
 
     lax.fori_loop(0, devices, contract, 0)
-    answer = jnp.zeros((devices, 128), F32)
-    for c, (idx, valid) in enumerate(((idx0, valid0), (idx1, valid1))):
-        tile_of = jnp.where(valid, idx // bands, -1)
+    answers = []
+    for c in range(2):
+        answer = jnp.zeros((devices, 128), F32)
         for f in range(GRADS):
             value = jnp.sum(jnp.sum(partial[c, f], axis=1), axis=1, keepdims=True)
-            answer = answer + jnp.where(lane == f * tiles + tile_of, value, 0.0)
-    values[...] = answer
-
-    def unfold(j, carry):
-        returned[j] = values[pl.ds(j, 1), :]
-        return carry
-
-    lax.fori_loop(0, devices, unfold, 0)
-    returning[me] = returned[me]
-
-    def sum_copy(peer, from_):
+            answer = jnp.where(lane == f, value, answer)
+        answers.append(answer)
+    mine_sums[...] = jnp.transpose(jnp.concatenate(answers, axis=0))[:8]
+    all_sums[chip] = mine_sums[...]
+
+    def chip_copy(other, from_):
         return pltpu.make_async_remote_copy(
-            src_ref=returned.at[peer],
-            dst_ref=returning.at[from_],
-            send_sem=send_r.at[peer],
-            recv_sem=recv_r.at[from_],
-            device_id=(me_sec, peer),
+            src_ref=mine_sums,
+            dst_ref=all_sums.at[from_],
+            send_sem=send_c.at[other],
+            recv_sem=recv_c.at[from_],
+            device_id=(me_sec, other * 2 + core),
             device_id_type=MESH,
         )
 
-    def send_sums(d, carry):
-        sum_copy(lax.rem(me + d, devices), me).start()
-        return carry
-
-    lax.fori_loop(1, devices, send_sums, 0)
-
-    def await_sums(d, carry):
-        j = lax.rem(me + d, devices)
-        sum_copy(j, j).wait_recv()
-        return carry
-
-    lax.fori_loop(1, devices, await_sums, 0)
-    own = own + jnp.sum(returning[...], axis=0)
-
-    payload[...] = own
+    def send_rows(d, carry):
+        chip_copy(lax.rem(chip + d, chips), chip).start()
+        return carry
+
+    lax.fori_loop(1, chips, send_rows, 0)
+
+    def await_rows(d, carry):
+        j = lax.rem(chip + d, chips)
+        chip_copy(j, j).wait_recv()
+        return carry
+
+    lax.fori_loop(1, chips, await_rows, 0)
+
+    row_id, lane_id = iota((8, 128), 0), iota((8, 128), 1)
+    left_side = lane_id < devices
+    by_tile = []
+    for t in range(tiles):
+        added = jnp.sum(jnp.where(home[...] == float(t), all_sums[...], 0.0), axis=0)
+        by_tile.append(added + pltpu.roll(added, devices, 1))
     place = me_sec * 2 + core
-    gathered_pair[place] = own
+    for h in range(2):
+        pair_sums[h] = jnp.where(left_side, by_tile[2 * h], by_tile[2 * h + 1])
+    all_pairs[place] = pair_sums[...]
 
     def pair_copy(n, peer, from_):
         return pltpu.make_async_remote_copy(
-            src_ref=payload,
-            dst_ref=gathered_pair.at[from_],
+            src_ref=pair_sums,
+            dst_ref=all_pairs.at[from_],
             send_sem=send_p.at[n],
             recv_sem=recv_p.at[from_],
             device_id=peer,
@@ -382,66 +439,38 @@
 
     for n, peer in enumerate(pair_peers):
         pair_copy(n, peer, place).start()
+    for ds in range(1, sections):
+        s = lax.rem(me_sec + ds, sections)
+        section_copy(ds, s).wait_recv()
     for n, peer in enumerate(pair_peers):
         pair_copy(n, peer, peer[0] * 2 + lax.rem(peer[1], 2)).wait_recv()
-    for n in range(2 * sections):
-        chip_rows[n : n + 1, :] = gathered_pair[n]
-    gathered[chip] = chip_rows[...]
-
-    def chip_copy(other, from_):
-        return pltpu.make_async_remote_copy(
-            src_ref=chip_rows,
-            dst_ref=gathered.at[from_],
-            send_sem=send_c.at[other],
-            recv_sem=recv_c.at[from_],
-            device_id=(me_sec, other * 2 + core),
-            device_id_type=MESH,
-        )
-
-    def send_rows(d, carry):
-        chip_copy(lax.rem(chip + d, chips), chip).start()
-        return carry
-
-    lax.fori_loop(1, chips, send_rows, 0)
-
-    def await_rows(d, carry):
-        j = lax.rem(chip + d, chips)
-        chip_copy(j, j).wait_recv()
-        return carry
-
-    lax.fori_loop(1, chips, await_rows, 0)
-    everyone = 2 * sections * chips
-    planes[...] = jnp.transpose(gathered[...].reshape(everyone, 128))
-
-    shape = (8, everyone)
-    lane_id = iota(shape, 1)
-    tile_id = iota(shape, 0)
-    pairs = 2 * sections
-    lane_chip, lane_sec, lane_core = lane_id // pairs, (lane_id % pairs) // 2, lane_id % 2
-    used = tile_id < tiles
-    right_side = [
-        jnp.where(used, planes[f * tiles : f * tiles + 8, :], 0.0) for f in range(GRADS)
-    ]
-    moment = [
-        planes[(GRADS + m) * tiles : (GRADS + m) * tiles + 8, :] for m in range(18)
-    ]
-    precond = [
-        jnp.where(used, 1.0 / (moment[moment_of(f, f)] + 4.0 * COUPLING), 0.0) for f in range(GRADS)
-    ]
-    has_next = ~((lane_chip == chips - 1) & (lane_core == 1)) | (tile_id < tiles - 1)
-    has_before = ~((lane_chip == 0) & (lane_core == 0)) | (tile_id > 0)
+    for s in range(sections):
+        for h in range(2):
+            right_v[2 * s + h] = all_pairs[2 * s, h] + all_pairs[2 * s + 1, h]
+
+    shape = (8, 128)
+    moment = [mom_all[:, :, m, :].reshape(shape) for m in range(18)]
+    right_side = [right_v[:, f, :] - moment[moment_of(f, 3)] for f in range(GRADS)]
+    precond = [1.0 / (moment[moment_of(f, f)] + 4.0 * COUPLING) for f in range(GRADS)]
+    upper_pair = (row_id & 1) == 1
+    device_id = lane_id & (devices - 1)
 
     def beside_of(d):
-        up = pltpu.roll(d, 7, 0)
-        over = pltpu.roll(d, tiles - 1, 0)
-        over = jnp.where(lane_core == 0, shifted(over, 1), shifted(over, pairs - 1))
-        after = jnp.where(used & has_next, jnp.where(tile_id == tiles - 1, over, up), 0.0)
-        down = pltpu.roll(d, 1, 0)
-        under = pltpu.roll(d, 8 - (tiles - 1), 0)
-        under = jnp.where(lane_core == 1, shifted(under, -1), shifted(under, 1 - pairs))
-        before = jnp.where(used & has_before, jnp.where(tile_id == 0, under, down), 0.0)
-        upper = jnp.where(lane_sec < sections - 1, shifted(d, 2), 0.0)
-        lower = jnp.where(lane_sec > 0, shifted(d, -2), 0.0)
+        across = pltpu.roll(d, devices, 1)
+        after = jnp.where(
+            upper_pair,
+            jnp.where(device_id < devices - 1, pltpu.roll(shifted(across, 1), 1, 0), 0.0),
+            pltpu.roll(across, 7, 0),
+        )
+        after = jnp.where(left_side, across, after)
+        before = jnp.where(
+            upper_pair,
+            pltpu.roll(across, 1, 0),
+            jnp.where(device_id > 0, pltpu.roll(shifted(across, -1), 7, 0), 0.0),
+        )
+        before = jnp.where(left_side, before, across)
+        upper = jnp.where(row_id < 6, pltpu.roll(d, 6, 0), 0.0)
+        lower = jnp.where(row_id >= 2, pltpu.roll(d, 2, 0), 0.0)
         return upper + lower + after + before
 
     def inner(left, right):
@@ -467,16 +496,19 @@
             ratio = following / current
             direction = [z + ratio * d for z, d in zip(scaled, direction)]
             current = following
-    my_lane = chip * pairs + place
+    own_device = device_id == me
+    first_lanes = iota((1, 128), 1)
     for f in range(GRADS):
-        column = jnp.sum(jnp.where(lane_id == my_lane, result[f], 0.0), axis=1, keepdims=True)
-        turned = jnp.where(iota((8, 128), 0) == iota((8, 128), 1), column, 0.0)
-        corr_ref[f] = jnp.sum(turned, axis=0, keepdims=True)[:, :tiles]
+        line = jnp.zeros((1, 128), F32)
+        for t in range(tiles):
+            spot = own_device & (row_id == me_sec * 2 + t // 2) & (left_side == (t % 2 == 0))
+            line = jnp.where(first_lanes == t, total(jnp.where(spot, result[f], 0.0)), line)
+        corr_ref[f] = line[:, :tiles]
 
     def sent(d, carry):
         peer = lax.rem(me + d, devices)
         band_copy(peer, me).wait_send()
-        sum_copy(peer, me).wait_send()
+        moment_copy(peer, me).wait_send()
         return carry
 
     lax.fori_loop(1, devices, sent, 0)
@@ -486,6 +518,8 @@
         return carry
 
     lax.fori_loop(1, chips, sent_rows, 0)
+    for ds in range(1, sections):
+        section_copy(ds, me_sec).wait_send()
     for n, peer in enumerate(pair_peers):
         pair_copy(n, peer, place).wait_send()
 
@@ -535,14 +569,17 @@
             vmem((bands, BAND, frame), BF16),
             vmem((bands, BAND, frame), BF16),
             vmem((2, GRADS, devices, 8, 128), F32),
-            vmem((devices, 128), F32),
+            vmem((chips, 8, 128), F32),
+            vmem((8, 128), F32),
+            vmem((chips, 8, 128), F32),
+            vmem((2, 8, 128), F32),
+            vmem((pairs, 2, 8, 128), F32),
+            vmem((2 * sections, 8, 128), F32),
+            vmem((1, 128), F32),
             vmem((devices, 1, 128), F32),
-            vmem((devices, 1, 128), F32),
-            vmem((1, 128), F32),
-            vmem((pairs, 1, 128), F32),
-            vmem((pairs, 128), F32),
-            vmem((chips, pairs, 128), F32),
-            vmem((128, chips * pairs), F32),
+            vmem((128, 128), F32),
+            vmem((2, 24, 128), F32),
+            vmem((sections, 2, 24, 128), F32),
             sem((3,)),
             sem,
             sem((tiles,)),
@@ -555,13 +592,15 @@
             sem,
             sem((devices,)),
             sem((devices,)),
+            sem((sections,)),
+            sem((sections,)),
             sem((pairs,)),
             sem((pairs,)),
             sem((chips,)),
             sem((chips,)),
         ],
         compiler_params=pltpu.CompilerParams(
-            collective_id=0, has_side_effects=True, vmem_limit_bytes=48 << 20
+            collective_id=0, has_side_effects=True, vmem_limit_bytes=63 << 20
         ),
     )(
         zoom[0],

time: 75.7 us -> 69.8 us (0.922)
  Pallas kernels: 68 us -> 64.5 us
  local copies, waits for them, and re-layouts: 6.76 us -> 4.44 us
    pallas_call x1, Pallas kernels: 68 us -> 64.5 us  [shards(): pl.pallas_call(functools.partial(kernel, sections, devices, tiles, source...]
    unnamed x13 -> x3, local copies, waits for them, and re-layouts: 6.67 us -> 3.73 us
where the time goes in v2:
time: 69.8 us; the launch traced here: 69.6 us
  Pallas kernels  64.5 us (92%)
  local copies, waits for them, and re-layouts  4.44 us (6%)
    pallas_call x1, Pallas kernels, shards(): pl.pallas_call(functools.partial(kernel, sections, devices, tiles, source...  64.5 us
    unnamed x3, local copies, waits for them, and re-layouts  3.73 us

profile of v2, /device:TPU:1, one launch (start us, length us, event | category | flops | bytes accessed | tf_op | source)
XLA Modules:
  0.0 69.6 jit_solution(5756436006909895427)
XLA Ops:
  0.6 0.8 %copy.10 = s32[1,256,16,1]{2,1,3,0:T(8,128)S(1)} copy(s32[1,256,16,1]{1,3,2,0:T(1,128)} %param.10) | data formatting | bytes 32768 | tf_op args[4]
  1.4 0.1 reshape.13
  1.5 0.6 pad.4.routes_hbm
  2.2 64.5 %shard_map.77 = (bf16[16,16,256]{2,1,0:T(8,128)(2,1)}, f32[6,1,4]{2,1,0:T(1,128)}) custom-call(f32[2,256]{1,0:T(2,128)} %bitcast.13, f32[2,256]{1,0:T(2,128)} %bitcast.14, s32[2,256]{1,0:T(2,128)} %bitcast.15, s32[64,128]{1,0:T(8,128)} %pad.4.routes_hbm, bf16[4,512,512]{2,1,0:T(8,128)(2,1)} %bitcast.10, bf16[16,16,256]{2,1,0:T(8,128)(2,1)} %bitcast.11), custom_call_target="tpu_custom_call" | custom-call | tf_op jit(solution)/shard_map/pallas_call | solution.py:545
  66.7 1.3 %copy.11 = f32[6,1,4]{0,2,1:T(4,128)} copy(f32[6,1,4]{2,1,0:T(1,128)} %get-tuple-element.9) | data formatting | bytes 192
  68.0 1.6 %copy.13 = bf16[1,1,256,256]{3,2,1,0:T(8,128)(2,1)} copy(bf16[1,1,256,256]{3,2,1,0:T(8,128)(2,1)} %bitcast.12) | data formatting | bytes 262144
